TPU v7x, 32 devices: a whole 2x2x4 slice. The times are simulated.
32 devices in a mesh: expert: 8 (over y, x, core), replica: 4 (over z).
Axes of the slice: x: 2, y: 2, z: 4, core: 2. Of those that a mesh axis runs over, the one named last changes fastest.
Arguments:
- tokens: bfloat16 [8192, 7168], P(('expert', 'replica')), may hold values from -40 to 40
- routes: int32 [8192, 8], P(('expert', 'replica')), may hold values from 0 to 255, all different within a row
- gate_weight: bfloat16 [7168, 4096], P(None, 'expert'), may hold values from -0.0625 to 0.0625
- up_weight: bfloat16 [7168, 4096], P(None, 'expert'), may hold values from -0.0625 to 0.0625
Outputs:
- calibrated: bfloat16 [512, 4096], P(('expert', 'replica'))
Inputs may be any that keep to these rules, and one draw needn't show every extreme that they name: `routes`: each row names 8 different experts of the layer, and every expert is named by some row.
All inputs are finite; a program needn't handle non-finite values.
Results may differ from a plain program's by a relative error of at most 0.001.
Values may be sent and summed in bfloat16 or wider, within the bound.
A program may use at most 128 MiB of HBM per device.

v0:
```python
import math

import jax
import jax.numpy as jnp
from jax import lax
from jax.sharding import PartitionSpec as P

D = 7168
HSPLIT = 4
CAP = 16
KMOM = 12
QITERS = 4


QUANTILE_LEVEL = 0.99
EPSILON = 1e-06


def build_slots(routes, experts):
    window = jnp.arange(experts, dtype=jnp.int32)
    naming = jnp.sum((routes[:, :, None] == window[None, None, :]).astype(jnp.int32), axis=1)
    before = jnp.cumsum(naming, axis=0) - naming
    positions = jnp.arange(CAP, dtype=jnp.int32)
    chosen = naming[:, :, None] * (before[:, :, None] == positions[None, None, :]).astype(jnp.int32)
    token_ids = jnp.arange(routes.shape[0], dtype=jnp.int32)
    picked = jnp.sum(chosen * token_ids[:, None, None], axis=0)
    filled = jnp.sum(chosen, axis=0)
    return (picked, filled)


def chebyshev_sums(scaled, occupied):
    previous = jnp.ones_like(scaled)
    current = scaled
    totals = [
        jnp.sum(occupied[:, None] * previous, axis=0),
        jnp.sum(occupied[:, None] * current, axis=0),
    ]
    for degree in range(2, KMOM):
        previous, current = (current, 2.0 * scaled * current - previous)
        totals.append(jnp.sum(occupied[:, None] * current, axis=0))
    return jnp.stack(totals[:KMOM])


def clip_fraction(moments, counted):
    coefficient = moments[1:] / counted[None, :]
    orders = jnp.arange(1, KMOM, dtype=jnp.float32)[:, None]
    angles = jnp.full(moments.shape[1:], 0.5 * math.pi, jnp.float32)
    for iteration in range(QITERS):
        lower_mass = (
            1.0
            - angles / math.pi
            - 2.0
            / math.pi
            * jnp.sum(coefficient * jnp.sin(orders * angles[None, :]) / orders, axis=0)
        )
        angles = angles + math.pi * (lower_mass - QUANTILE_LEVEL)
    return 0.5 * (1.0 + jnp.cos(angles))


def shards(tokens, routes, gate_weight, up_weight):
    devices_e = lax.axis_size("expert")
    experts = devices_e // HSPLIT
    shard_width = gate_weight.shape[1]
    picked, filled = build_slots(routes, experts)
    occupied = filled.astype(jnp.bfloat16)
    gathered = jnp.take(tokens, picked.reshape(-1), axis=0).reshape(experts, CAP, D)
    gathered = gathered * occupied[:, :, None]
    outgoing = jnp.repeat(gathered, HSPLIT, axis=0)
    presence = jnp.repeat(occupied, HSPLIT, axis=0)
    received = lax.all_to_all(outgoing, "expert", split_axis=0, concat_axis=0, tiled=True)
    flat_rows = received.reshape(-1, D)
    gate_act = jnp.dot(flat_rows, gate_weight, preferred_element_type=jnp.float32)
    up_act = jnp.dot(flat_rows, up_weight, preferred_element_type=jnp.float32)
    hidden = jax.nn.silu(gate_act) * up_act
    hidden, present = (
        hidden.reshape(received.shape[:-1] + (shard_width,)),
        lax.all_to_all(presence, "expert", split_axis=0, concat_axis=0, tiled=True),
    )
    magnitude = jnp.abs(hidden)
    ceiling = lax.pmax(jnp.max(magnitude, axis=(0, 1)), "replica") + EPSILON
    scaled = 2.0 * magnitude / ceiling - 1.0
    local_sums = chebyshev_sums(
        scaled.reshape(-1, shard_width), present.reshape(-1).astype(jnp.float32)
    )
    moments = lax.psum(local_sums, "replica")
    clip_level = ceiling * clip_fraction(moments, moments[0])
    calibrated = (jnp.clip(hidden, -clip_level, clip_level) / ceiling).astype(jnp.bfloat16)
    returned = lax.all_to_all(calibrated, "expert", split_axis=0, concat_axis=2, tiled=True)
    return returned.reshape(CAP, experts * HSPLIT * shard_width)


def solution(mesh):
    in_specs = (
        P(("expert", "replica"), None),
        P(("expert", "replica"), None),
        P(None, "expert"),
        P(None, "expert"),
    )
    out_specs = P(("expert", "replica"), None)
    return jax.shard_map(shards, mesh=mesh, in_specs=in_specs, out_specs=out_specs, check_vma=False)
```

profile of v0, /device:TPU:0, one launch (start us, length us, event | category | flops | bytes accessed | tf_op | source)
XLA Modules:
  0.0 88.1 jit_solution(15963084966948955778)
XLA Ops:
  0.0 0.7 convert_reduce_fusion
  0.7 0.6 reduce-window.6
  1.3 0.2 slice_reduce_fusion
  1.6 0.2 reduce-window.9
  1.8 0.2 select_reduce_fusion
  2.0 0.6 copy.18
  2.6 5.2 %all-to-all-start.1 = ((bf16[8,1,16]{2,1,0:T(2,128)(2,1)}), bf16[8,1,16]{2,1,0:T(2,128)(2,1)S(1)}, u32[]{:S(2)}, u32[]{:S(2)}) async-start(bf16[8,1,16]{2,1,0:T(2,128)(2,1)} %copy.18), calls=%async_computation.1 | async-start | bytes 8192 | tf_op jit(solution)/shard_map/all_to_all | solution.py:77
  7.9 3.8 %gather_fusion = bf16[32,7168]{1,0:T(8,128)(2,1)S(1)} fusion(bf16[256,7168]{1,0:T(8,128)(2,1)} %param.4, s32[1024]{0:T(1024)S(1)} %pad_clamp_fusion), kind=kCustom, calls=%fused_computation | custom fusion | bytes 917632 | tf_op jit(solution)/shard_map/jit(_take)/gather | solution.py:66
  11.8 0.6 all-to-all-done.1
  12.4 1.4 %broadcast_in_dim.20 = bf16[2,4,16,7168]{3,2,1,0:T(8,128)(2,1)} broadcast(bf16[2,16,7168]{2,1,0:T(8,128)(2,1)S(1)} %select_multiply_fusion), dimensions={0,2,3} | broadcast | bytes 2293760 | tf_op jit(solution)/shard_map/broadcast_in_dim | solution.py:68
  13.8 3.6 %all-to-all-start = ((bf16[8,16,7168]{2,1,0:T(8,128)(2,1)}), bf16[8,16,7168]{2,1,0:T(8,128)(2,1)S(1)}, u32[]{:S(2)}, u32[]{:S(2)}) async-start(bf16[8,16,7168]{2,1,0:T(8,128)(2,1)} %bitcast.45), calls=%async_computation | async-start | bytes 3670016 | tf_op jit(solution)/shard_map/all_to_all | solution.py:70
  17.5 0.6 convert_reduce_fusion.1
  18.2 23.0 %all-to-all-done = bf16[8,16,7168]{2,1,0:T(8,128)(2,1)S(1)} async-done(((bf16[8,16,7168]{2,1,0:T(8,128)(2,1)}), bf16[8,16,7168]{2,1,0:T(8,128)(2,1)S(1)}, u32[]{:S(2)}, u32[]{:S(2)}) %all-to-all-start) | async-done | bytes 1835040 | tf_op jit(solution)/shard_map/all_to_all | solution.py:70
  41.2 4.2 %fusion.8 = f32[128,512]{1,0:T(8,128)S(1)} fusion(bf16[128,7168]{1,0:T(8,128)(2,1)S(1)} %bitcast.43, bf16[7168,512]{1,0:T(8,128)(2,1)} %param.6), kind=kOutput, calls=%fused_computation.60 | convolution fusion | flops 939524096 | bytes 9437184 | tf_op jit(solution)/shard_map/dot_general | solution.py:72
  45.5 4.2 %abs_reduce_fusion = (f32[512]{0:T(512)S(1)}, f32[128,512]{1,0:T(8,128)S(1)}) fusion(bf16[128,7168]{1,0:T(8,128)(2,1)S(1)} %bitcast.44, bf16[7168,512]{1,0:T(8,128)(2,1)} %param.7, f32[128,512]{1,0:T(8,128)S(1)} %fusion.8), kind=kOutput, calls=%fused_computation.25 | convolution fusion | flops 939982336 | bytes 9701376 | tf_op jit(solution)/shard_map/dot_general | solution.py:73
  49.7 12.0 %pmax.7 = f32[512]{0:T(512)S(1)} all-reduce(f32[512]{0:T(512)S(1)} %get-tuple-element.22), channel_id=1, replica_groups=mesh['expert'=8,'replica'=4] {'replica'}, use_global_device_ids=true, to_apply=%region_6.7 | all-reduce | flops 512 | bytes 4096 | tf_op jit(solution)/shard_map/pmax | solution.py:80
  61.7 0.5 multiply_reduce_fusion
  62.1 0.6 stack.39
  62.9 15.8 %psum.7 = f32[12,512]{1,0:T(8,128)S(1)} all-reduce(f32[12,512]{1,0:T(8,128)S(1)} %stack.51), channel_id=1, replica_groups=mesh['expert'=8,'replica'=4] {'replica'}, use_global_device_ids=true, to_apply=%region_19.20 | all-reduce | flops 6144 | bytes 49152 | tf_op jit(solution)/shard_map/psum | solution.py:85
  78.8 0.2 fusion.2
  79.0 0.2 fusion.3
  79.2 0.2 fusion.4
  79.6 7.9 %all_to_all.29 = bf16[8,16,512]{2,1,0:T(8,128)(2,1)S(1)} all-to-all(bf16[8,16,512]{2,1,0:T(8,128)(2,1)S(1)} %divide_convert_fusion), channel_id=1, replica_groups=mesh['expert'=8,'replica'=4] {'expert'}, dimensions={0} | all-to-all | bytes 262144 | tf_op jit(solution)/shard_map/all_to_all | solution.py:88
  87.5 0.7 copy.21
  (22 shorter events, 0.7 us)
Async XLA Ops:
  2.6 9.8 %all-to-all-start.1 = ((bf16[8,1,16]{2,1,0:T(2,128)(2,1)}), bf16[8,1,16]{2,1,0:T(2,128)(2,1)S(1)}, u32[]{:S(2)}, u32[]{:S(2)}) async-start(bf16[8,1,16]{2,1,0:T(2,128)(2,1)} %copy.18), calls=%async_computation.1 | async-start | bytes 8192 | tf_op jit(solution)/shard_map/all_to_all | solution.py:77
  13.8 27.4 %all-to-all-start = ((bf16[8,16,7168]{2,1,0:T(8,128)(2,1)}), bf16[8,16,7168]{2,1,0:T(8,128)(2,1)S(1)}, u32[]{:S(2)}, u32[]{:S(2)}) async-start(bf16[8,16,7168]{2,1,0:T(8,128)(2,1)} %bitcast.45), calls=%async_computation | async-start | bytes 3670016 | tf_op jit(solution)/shard_map/all_to_all | solution.py:70
where the time goes:
time: 88.6 us; the launch traced here: 88.1 us
  blocking collectives  35.6 us (40%)
  waiting for transfers between devices  23.7 us (27%)
  starting transfers between devices  8.79 us (10%)
  matrix products  8.45 us (10%)
  local copies, waits for them, and re-layouts  7.57 us (9%)
  other arithmetic  3.88 us (4%)
    all_to_all x1, waiting for transfers between devices, shards(): lax.all_to_all(outgoing, 'expert', split_axis=0, concat_axis=0, tiled=True)  23 us
    psum x1, blocking collectives, shards(): moments = lax.psum(local_sums, 'replica')  15.8 us
    pmax x1, blocking collectives, shards(): ceiling = lax.pmax(jnp.max(magnitude, axis=(0, 1)), 'replica') + EPSILON  12 us
    all_to_all x1, blocking collectives, shards(): lax.all_to_all(calibrated, 'expert', split_axis=0, concat_axis=2, tiled=T...  7.89 us
    all_to_all x1, starting transfers between devices, shards(): lax.all_to_all(presence, 'expert', split_axis=0, concat_axis=0, tiled=True)  5.2 us
    dot_general x1, matrix products, shards(): up_act = jnp.dot(flat_rows, up_weight, preferred_element_type=jnp.float32)  4.23 us
    dot_general x1, matrix products, shards(): jnp.dot(flat_rows, gate_weight, preferred_element_type=jnp.float32)  4.22 us
    gather x1, local copies, waits for them, and re-layouts, shards(): jnp.take(tokens, picked.reshape(-1), axis=0).reshape(experts, CAP, D)  3.76 us
  transfers between devices with their start and end apart: 2, of which 2 were waited for; matrix products, arithmetic and copies ran while one was open for 5% of the time, Pallas kernels for 0%

commit v1 on v0

v1 whole, which is shorter than its diff:
```python
import functools
import math

import jax
import jax.numpy as jnp
from jax import lax
from jax.experimental import pallas as pl
from jax.experimental.pallas import tpu as pltpu
from jax.sharding import PartitionSpec as P

HSPLIT = 4
CAP = 16
KMOM = 12
QITERS = 4
LANES = 128
CHUNK = 1024
ROWS = 32

QUANTILE_LEVEL = 0.99
EPSILON = 1e-06
MESH = pl.DeviceIdType.MESH

PI_HIGH = 3.140625
PI_LOW = math.pi - PI_HIGH
SIN_TERMS = [(-1.0) ** i / math.factorial(2 * i + 1) for i in range(7)]
COS_TERMS = [(-1.0) ** i / math.factorial(2 * i) for i in range(8)]


def horner(square, terms):
    total = jnp.full_like(square, terms[-1])
    for term in terms[-2::-1]:
        total = total * square + term
    return total


def sin_cos(angle):
    turns = jnp.floor(angle * (1.0 / math.pi) + 0.5)
    rest = (angle - turns * PI_HIGH) - turns * PI_LOW
    sign = 1.0 - 2.0 * (turns - 2.0 * jnp.floor(turns * 0.5))
    square = rest * rest
    return sign * rest * horner(square, SIN_TERMS), sign * horner(square, COS_TERMS)


def clip_fraction(coefficient):
    start = (1.0 - QUANTILE_LEVEL) * math.pi
    total = jnp.zeros_like(coefficient[0])
    for k in range(1, KMOM, 2):
        total = total + coefficient[k - 1] * ((1.0 if k % 4 == 1 else -1.0) / k)
    angle = start - 2.0 * total
    for _ in range(QITERS - 1):
        sine, cosine = sin_cos(angle)
        double = 2.0 * cosine
        before, current = jnp.zeros_like(sine), sine
        total = jnp.zeros_like(sine)
        for k in range(1, KMOM):
            total = total + coefficient[k - 1] * (current * (1.0 / k))
            before, current = current, double * current - before
        angle = start - 2.0 * total
    return 0.5 * (1.0 + sin_cos(angle)[1])


def rebase(moments, ratio):
    shift = ratio - 1.0
    before = moments
    current = [
        0.5 * ratio * (before[j + 1] + before[abs(j - 1)]) + shift * before[j]
        for j in range(KMOM - 1)
    ]
    out = [current[0]]
    twice = 2.0 * shift
    for k in range(1, KMOM - 1):
        following = [
            ratio * (current[j + 1] + current[abs(j - 1)]) + twice * current[j] - before[j]
            for j in range(KMOM - 1 - k)
        ]
        before, current = current, following
        out.append(current[0])
    return out


def kernel(
    devices, replicas, chunks,
    tok, rt, wg, wu, out,
    T, RT, SEL, Y, OY, X, OX, WG, WU, AG, AU, H, SK, CNT, RES,
    tok_sem, rt_sem, wg_sem, wu_sem,
    x_send, x_recv, o_send, o_recv, f_send, f_recv, fo_sem,
    s_send, s_recv, n_send, n_recv, r_send, r_recv, own_sem,
):
    groups = devices // HSPLIT
    half = devices // 2 * CAP
    width = WG.shape[1]
    tiles = width // LANES
    rows = devices * CAP
    me = lax.axis_index("expert")
    z = lax.axis_index("replica")
    c = me % 2
    p = (me // 2) % 2
    a = me // HSPLIT
    partner = me + 1 - 2 * c

    def pos(j):
        return (j % 2) * (devices // 2) + j // 2

    def other(dg, dp, dc):
        return HSPLIT * ((a + dg) % groups) + 2 * ((p + dp) % 2) + (c + dc) % 2

    combos = [(dg, dp) for dg in range(groups) for dp in range(2) if (dg, dp) != (0, 0)]
    combos = combos[::-1]
    alls = [
        (dg, dp, dc)
        for dg in range(groups) for dp in range(2) for dc in range(2)
        if (dg, dp, dc) != (0, 0, 0)
    ]

    def block(j):
        return pl.ds(pl.multiple_of(pos(j) * CAP, CAP), CAP)

    def load_tokens(ch):
        return pltpu.make_async_copy(
            tok.at[:, pl.ds(pl.multiple_of(ch * CHUNK, CHUNK), CHUNK)], T.at[ch], tok_sem.at[ch])

    def load_weights(ch):
        part = pl.ds(pl.multiple_of(ch * CHUNK, CHUNK), CHUNK)
        return (
            pltpu.make_async_copy(wg.at[part], WG.at[part], wg_sem.at[ch]),
            pltpu.make_async_copy(wu.at[part], WU.at[part], wu_sem.at[ch]),
        )

    load_routes = pltpu.make_async_copy(rt, RT, rt_sem)
    load_routes.start()
    for ch in range(chunks):
        load_tokens(ch).start()

    barrier = pltpu.get_barrier_semaphore()
    for combo in alls:
        pl.semaphore_signal(barrier, inc=1, device_id=(other(*combo), z), device_id_type=MESH)
    for dz in range(1, replicas):
        pl.semaphore_signal(
            barrier, inc=1, device_id=(me, (z + dz) % replicas), device_id_type=MESH)

    for ch in range(chunks):
        for copy in load_weights(ch):
            copy.start()

    load_routes.wait()
    routes = RT[...]
    count = routes.shape[1]
    t_from = lax.broadcasted_iota(jnp.int32, (count, count), 0)
    t_to = lax.broadcasted_iota(jnp.int32, (count, count), 1)
    earlier = jnp.where(t_from < t_to, 1.0, 0.0).astype(jnp.bfloat16)
    named = [
        jnp.sum(jnp.where(routes == (a + dg) % groups, 1.0, 0.0), axis=0, keepdims=True)
        for dg in range(groups)
    ]
    table = jnp.concatenate(
        [jnp.broadcast_to(n, (CAP, count)) for n in named], axis=0)
    before = jnp.dot(table.astype(jnp.bfloat16), earlier, preferred_element_type=jnp.float32)
    slot = (lax.broadcasted_iota(jnp.int32, (groups * CAP, count), 0) % CAP).astype(jnp.float32)
    picks = jnp.where(before == slot, table, 0.0)
    SEL[...] = picks.astype(jnp.bfloat16)
    filled = jnp.broadcast_to(
        jnp.sum(picks, axis=1, keepdims=True), (groups * CAP, LANES)).astype(jnp.bfloat16)
    OY[...] = filled
    OX[block(me), :] = filled[:CAP]

    def gather(ch):
        load_tokens(ch).wait()
        picked = jnp.dot(
            SEL[...], T[ch], preferred_element_type=jnp.float32).astype(jnp.bfloat16)
        Y[ch] = picked
        X[ch, block(me), :] = picked[:CAP]

    def send_rows(ch, i):
        dg, dp = combos[i]
        return pltpu.make_async_remote_copy(
            src_ref=Y.at[ch, pl.ds(dg * CAP, CAP), :], dst_ref=X.at[ch, block(me), :],
            send_sem=x_send.at[ch, i], recv_sem=x_recv.at[ch, i],
            device_id=(other(dg, dp, 0), z), device_id_type=MESH)

    def send_filled(i):
        dg, dp = combos[i]
        return pltpu.make_async_remote_copy(
            src_ref=OY.at[pl.ds(dg * CAP, CAP), :], dst_ref=OX.at[block(me), :],
            send_sem=o_send.at[i], recv_sem=o_recv.at[i],
            device_id=(other(dg, dp, 0), z), device_id_type=MESH)

    def forward_rows(ch):
        part = pl.ds(pl.multiple_of(c * half, half), half)
        return pltpu.make_async_remote_copy(
            src_ref=X.at[ch, part, :], dst_ref=X.at[ch, part, :],
            send_sem=f_send.at[ch], recv_sem=f_recv.at[ch],
            device_id=(partner, z), device_id_type=MESH)

    def forward_filled():
        part = pl.ds(pl.multiple_of(c * half, half), half)
        return pltpu.make_async_remote_copy(
            src_ref=OX.at[part, :], dst_ref=OX.at[part, :],
            send_sem=fo_sem.at[0], recv_sem=fo_sem.at[1],
            device_id=(partner, z), device_id_type=MESH)

    gather(0)
    pl.semaphore_wait(barrier, len(alls) + replicas - 1)
    for i in range(len(combos)):
        send_filled(i).start()

    def sending(ch, _):
        gather(ch + 1)
        for i in range(len(combos)):
            send_rows(ch, i).start()
        return 0

    lax.fori_loop(0, chunks - 1, sending, 0)
    for i in range(len(combos)):
        send_rows(chunks - 1, i).start()

    for i in range(len(combos)):
        send_filled(i).wait_recv()
    forward_filled().start()

    def collect(ch):
        for i in range(len(combos)):
            send_rows(ch, i).wait_recv()
        forward_rows(ch).start()

    def multiply(ch, first):
        forward_rows(ch).wait_recv()
        for copy in load_weights(ch):
            copy.wait()
        part = pl.ds(pl.multiple_of(ch * CHUNK, CHUNK), CHUNK)
        x = X[ch]
        for W, A in ((WG, AG), (WU, AU)):
            product = jnp.dot(x, W[part, :], preferred_element_type=jnp.float32)
            A[...] = product if first else A[...] + product

    collect(0)
    collect(1)
    multiply(0, True)

    forward_filled().wait()
    total = jnp.sum(OX[...].astype(jnp.float32), axis=0, keepdims=True)
    CNT[z] = jnp.broadcast_to(total, (8, LANES))

    def step(ch, _):
        collect(ch + 1)
        multiply(ch, False)
        return 0

    lax.fori_loop(1, chunks - 1, step, 0)

    def send_count(dz):
        return pltpu.make_async_remote_copy(
            src_ref=CNT.at[z], dst_ref=CNT.at[z],
            send_sem=n_send.at[dz - 1], recv_sem=n_recv.at[dz - 1],
            device_id=(me, (z + dz) % replicas), device_id_type=MESH)

    for dz in range(1, replicas):
        send_count(dz).start()
    multiply(chunks - 1, False)

    def activate(i, top):
        part = pl.ds(pl.multiple_of(i * ROWS, ROWS), ROWS)
        g = AG[part, :]
        h = g / (1.0 + jnp.exp(-g)) * AU[part, :]
        H[part, :] = h
        return jnp.maximum(top, jnp.max(jnp.abs(h).reshape(ROWS // 8, 8, width), axis=0))

    top = lax.fori_loop(0, rows // ROWS, activate, jnp.zeros((8, width), jnp.float32))
    ceiling = jnp.max(top, axis=0, keepdims=True) + EPSILON
    scale = 2.0 / ceiling
    for l in range(tiles):
        lanes = slice(l * LANES, (l + 1) * LANES)
        scale_l = scale[:, lanes]

        def sketch(i, sums):
            part = pl.ds(pl.multiple_of(i * ROWS, ROWS), ROWS)
            scaled = jnp.abs(H[part, lanes]) * scale_l - 1.0
            double = 2.0 * scaled
            previous = OX[part, :].astype(jnp.float32)
            current = previous * scaled
            new = []
            for k in range(KMOM - 1):
                new.append(sums[k] + jnp.sum(current.reshape(ROWS // 8, 8, LANES), axis=0))
                previous, current = current, double * current - previous
            return tuple(new)

        zero = jnp.zeros((8, LANES), jnp.float32)
        sums = lax.fori_loop(0, rows // ROWS, sketch, (zero,) * (KMOM - 1))
        SK[z, l:l + 1, :] = ceiling[:, lanes]
        for k in range(1, KMOM):
            SK[z, k * tiles + l:k * tiles + l + 1, :] = jnp.sum(
                sums[k - 1], axis=0, keepdims=True)

    def send_sketch(dz):
        return pltpu.make_async_remote_copy(
            src_ref=SK.at[z], dst_ref=SK.at[z],
            send_sem=s_send.at[dz - 1], recv_sem=s_recv.at[dz - 1],
            device_id=(me, (z + dz) % replicas), device_id_type=MESH)

    for dz in range(1, replicas):
        send_sketch(dz).start()
    for dz in range(1, replicas):
        send_count(dz).wait()
    for dz in range(1, replicas):
        send_sketch(dz).wait()

    def across(k):
        return [SK[r, k * tiles:(k + 1) * tiles, :] for r in range(replicas)]

    local = across(0)
    common = functools.reduce(jnp.maximum, local)
    ratio = jnp.concatenate([value / common for value in local], axis=0)
    moments = [jnp.concatenate([CNT[r, :tiles, :] for r in range(replicas)], axis=0)]
    moments += [jnp.concatenate(across(k), axis=0) for k in range(1, KMOM)]

    def added(value):
        return functools.reduce(
            jnp.add, [value[r * tiles:(r + 1) * tiles] for r in range(replicas)])

    weight = 1.0 / added(moments[0])
    level = clip_fraction([added(value) * weight for value in rebase(moments, ratio)])
    level = common * level
    inverse = 1.0 / common

    for l in range(tiles):
        lanes = slice(l * LANES, (l + 1) * LANES)
        bound = level[l:l + 1]
        factor = inverse[l:l + 1]

        def finish(i, _):
            part = pl.ds(pl.multiple_of(i * ROWS, ROWS), ROWS)
            h = jnp.minimum(jnp.maximum(H[part, lanes], -bound), bound)
            RES[part, lanes] = (h * factor).astype(jnp.bfloat16)
            return 0

        lax.fori_loop(0, rows // ROWS, finish, 0)

    mine = pl.ds(pl.multiple_of(me * width, width), width)

    def send_result(i):
        j = other(*alls[i])
        return pltpu.make_async_remote_copy(
            src_ref=RES.at[block(j), :], dst_ref=out.at[:, mine],
            send_sem=r_send.at[i], recv_sem=r_recv.at[i],
            device_id=(j, z), device_id_type=MESH)

    for i in range(len(alls))[::-1]:
        send_result(i).start()
    keep = pltpu.make_async_copy(RES.at[block(me), :], out.at[:, mine], own_sem)
    keep.start()

    def drain(ch, _):
        for i in range(len(combos)):
            send_rows(ch, i).wait_send()
        forward_rows(ch).wait_send()
        return 0

    lax.fori_loop(0, chunks, drain, 0)
    for i in range(len(combos)):
        send_filled(i).wait_send()
    keep.wait()
    for i in range(len(alls)):
        send_result(i).wait()


def shards(tokens, routes, gate_weight, up_weight):
    devices = lax.axis_size("expert")
    replicas = lax.axis_size("replica")
    groups = devices // HSPLIT
    count, depth = tokens.shape
    width = gate_weight.shape[1]
    chunks = depth // CHUNK
    rows = devices * CAP
    near = devices // 2 - 1
    tiles = width // LANES
    bf16, f32 = jnp.bfloat16, jnp.float32
    dma = pltpu.SemaphoreType.DMA
    anywhere = pl.BlockSpec(memory_space=pl.ANY)
    return pl.pallas_call(
        functools.partial(kernel, devices, replicas, chunks),
        out_shape=jax.ShapeDtypeStruct((CAP, devices * width), bf16),
        in_specs=[anywhere] * 4,
        out_specs=anywhere,
        scratch_shapes=[
            pltpu.VMEM((chunks, count, CHUNK), bf16),
            pltpu.VMEM((routes.shape[1], count), jnp.int32),
            pltpu.VMEM((groups * CAP, count), bf16),
            pltpu.VMEM((chunks, groups * CAP, CHUNK), bf16),
            pltpu.VMEM((groups * CAP, LANES), bf16),
            pltpu.VMEM((chunks, rows, CHUNK), bf16),
            pltpu.VMEM((rows, LANES), bf16),
            pltpu.VMEM((depth, width), bf16),
            pltpu.VMEM((depth, width), bf16),
            pltpu.VMEM((rows, width), f32),
            pltpu.VMEM((rows, width), f32),
            pltpu.VMEM((rows, width), f32),
            pltpu.VMEM((replicas, KMOM * tiles, LANES), f32),
            pltpu.VMEM((replicas, 8, LANES), f32),
            pltpu.VMEM((rows, width), bf16),
            dma((chunks,)), dma(()), dma((chunks,)), dma((chunks,)),
            dma((chunks, near)), dma((chunks, near)), dma((near,)), dma((near,)),
            dma((chunks,)), dma((chunks,)), dma((2,)),
            dma((replicas - 1,)), dma((replicas - 1,)),
            dma((replicas - 1,)), dma((replicas - 1,)),
            dma((devices - 1,)), dma((devices - 1,)), dma(()),
        ],
        compiler_params=pltpu.CompilerParams(
            collective_id=0, has_side_effects=True, vmem_limit_bytes=60 * 1024 * 1024),
    )(tokens, routes.T, gate_weight, up_weight)


def solution(mesh):
    in_specs = (
        P(("expert", "replica"), None),
        P(("expert", "replica"), None),
        P(None, "expert"),
        P(None, "expert"),
    )
    out_specs = P(("expert", "replica"), None)
    return jax.shard_map(shards, mesh=mesh, in_specs=in_specs, out_specs=out_specs, check_vma=False)
```

time: 88.6 us -> 30.5 us (0.34)
  blocking collectives: 35.6 us -> 0 us
  Pallas kernels: 0 us -> 28.8 us
  waiting for transfers between devices: 23.7 us -> 0 us
  starting transfers between devices: 8.79 us -> 0 us
  matrix products: 8.45 us -> 0 us
  local copies, waits for them, and re-layouts: 7.57 us -> 1.57 us
  other arithmetic: 3.88 us -> 0 us
    pallas_call x0 -> x1, Pallas kernels: none -> 28.8 us  [shards(): pl.pallas_call(functools.partial(kernel, devices, replicas, chunks), out_...]
    all_to_all x2 -> x0, waiting for transfers between devices: 23.7 us -> none  [the longest x1 23 us: shards(): lax.all_to_all(outgoing, 'expert', split_axis=0, concat_axis=0, tiled=True)]
    psum x1 -> x0, blocking collectives: 15.8 us -> none  [shards(): moments = lax.psum(local_sums, 'replica')]
    pmax x1 -> x0, blocking collectives: 12 us -> none  [shards(): ceiling = lax.pmax(jnp.max(magnitude, axis=(0, 1)), 'replica') + EPSILON]
    all_to_all x2 -> x0, starting transfers between devices: 8.79 us -> none  [the longest x1 5.2 us: shards(): lax.all_to_all(presence, 'expert', split_axis=0, concat_axis=0, tiled=True)]
    dot_general x2 -> x0, matrix products: 8.45 us -> none  [the longest x1 4.23 us: shards(): up_act = jnp.dot(flat_rows, up_weight, preferred_element_type=jnp.float32)]
    all_to_all x1 -> x0, blocking collectives: 7.89 us -> none  [shards(): lax.all_to_all(calibrated, 'expert', split_axis=0, concat_axis=2, tiled=T...]
    gather x1 -> x0, local copies, waits for them, and re-layouts: 3.76 us -> none  [shards(): jnp.take(tokens, picked.reshape(-1), axis=0).reshape(experts, CAP, D)]
  transfers between devices with their start and end apart: 2 -> 0, of which waited for: 2 -> 0; matrix products, arithmetic and copies ran while one was open for 5% -> 0% of each run, Pallas kernels for 0% -> 0%
where the time goes in v1:
time: 30.5 us; the launch traced here: 30.3 us
  Pallas kernels  28.8 us (94%)
  local copies, waits for them, and re-layouts  1.57 us (5%)
    pallas_call x1, Pallas kernels, shards(): pl.pallas_call(functools.partial(kernel, devices, replicas, chunks), out_...  28.8 us
    unnamed x1, local copies, waits for them, and re-layouts  1.57 us

profile of v1, /device:TPU:0, one launch (start us, length us, event | category | flops | bytes accessed | tf_op | source)
XLA Modules:
  0.0 30.3 jit_solution(10098697075260197920)
XLA Ops:
  0.0 28.8 %shard_map.46 = bf16[16,4096]{1,0:T(8,128)(2,1)} custom-call(bf16[256,7168]{1,0:T(8,128)(2,1)} %tok.1, s32[8,256]{1,0:T(8,128)} %bitcast.1, bf16[7168,512]{1,0:T(8,128)(2,1)} %wg.1, bf16[7168,512]{1,0:T(8,128)(2,1)} %wu.1), custom_call_target="tpu_custom_call" | custom-call | tf_op jit(solution)/shard_map/pallas_call | solution.py:378
  28.8 1.6 %copy.6 = bf16[16,4096]{1,0:T(8,128)(2,1)} copy(bf16[16,4096]{1,0:T(8,128)(2,1)} %shard_map.46) | data formatting | bytes 262144

commit v2 on v1

--- a/solution.py
+++ b/solution.py
@@ -13,7 +13,7 @@
 KMOM = 12
 QITERS = 4
 LANES = 128
-CHUNK = 1024
+CHUNK = 512
 ROWS = 32
 
 QUANTILE_LEVEL = 0.99
@@ -80,11 +80,11 @@
 
 def kernel(
     devices, replicas, chunks,
-    tok, rt, wg, wu, out,
-    T, RT, SEL, Y, OY, X, OX, WG, WU, AG, AU, H, SK, CNT, RES,
+    tok, rt, wg, wu, HB, LV,
+    T, RT, SEL, Y, OY, X, OX, WG, WU, AG, AU, H, SK, CNT, LS,
     tok_sem, rt_sem, wg_sem, wu_sem,
     x_send, x_recv, o_send, o_recv, f_send, f_recv, fo_sem,
-    s_send, s_recv, n_send, n_recv, r_send, r_recv, own_sem,
+    s_send, s_recv, n_send, n_recv, h_send, h_recv, l_send, l_recv, own_sem,
 ):
     groups = devices // HSPLIT
     half = devices // 2 * CAP
@@ -267,6 +267,31 @@
     top = lax.fori_loop(0, rows // ROWS, activate, jnp.zeros((8, width), jnp.float32))
     ceiling = jnp.max(top, axis=0, keepdims=True) + EPSILON
     scale = 2.0 / ceiling
+    mine = pl.ds(pl.multiple_of(me * width, width), width)
+
+    def send_hidden(i):
+        j = other(*alls[i])
+        return pltpu.make_async_remote_copy(
+            src_ref=H.at[block(j), :], dst_ref=HB.at[:, mine],
+            send_sem=h_send.at[i], recv_sem=h_recv.at[i],
+            device_id=(j, z), device_id_type=MESH)
+
+    def send_level(i):
+        return pltpu.make_async_remote_copy(
+            src_ref=LS, dst_ref=LV.at[:, mine],
+            send_sem=l_send.at[i], recv_sem=l_recv.at[i],
+            device_id=(other(*alls[i]), z), device_id_type=MESH)
+
+    def send_sketch(dz, part):
+        return pltpu.make_async_remote_copy(
+            src_ref=SK.at[z, part], dst_ref=SK.at[z, part],
+            send_sem=s_send.at[dz - 1, part], recv_sem=s_recv.at[dz - 1, part],
+            device_id=(me, (z + dz) % replicas), device_id_type=MESH)
+
+    keep_hidden = pltpu.make_async_copy(H.at[block(me), :], HB.at[:, mine], own_sem.at[0])
+    keep_level = pltpu.make_async_copy(LS, LV.at[:, mine], own_sem.at[1])
+    pair = tiles // 2
+
     for l in range(tiles):
         lanes = slice(l * LANES, (l + 1) * LANES)
         scale_l = scale[:, lanes]
@@ -285,26 +310,32 @@
 
         zero = jnp.zeros((8, LANES), jnp.float32)
         sums = lax.fori_loop(0, rows // ROWS, sketch, (zero,) * (KMOM - 1))
-        SK[z, l:l + 1, :] = ceiling[:, lanes]
+        at = l % pair
+        SK[z, l // pair, at:at + 1, :] = ceiling[:, lanes]
         for k in range(1, KMOM):
-            SK[z, k * tiles + l:k * tiles + l + 1, :] = jnp.sum(
+            SK[z, l // pair, k * pair + at:k * pair + at + 1, :] = jnp.sum(
                 sums[k - 1], axis=0, keepdims=True)
-
-    def send_sketch(dz):
-        return pltpu.make_async_remote_copy(
-            src_ref=SK.at[z], dst_ref=SK.at[z],
-            send_sem=s_send.at[dz - 1], recv_sem=s_recv.at[dz - 1],
-            device_id=(me, (z + dz) % replicas), device_id_type=MESH)
+        if l == pair:
+            for dz in range(1, replicas):
+                send_sketch(dz, 0).start()
+            for i in range(len(alls))[::-1]:
+                send_hidden(i).start()
+            keep_hidden.start()
 
     for dz in range(1, replicas):
-        send_sketch(dz).start()
+        send_sketch(dz, 1).start()
     for dz in range(1, replicas):
         send_count(dz).wait()
     for dz in range(1, replicas):
-        send_sketch(dz).wait()
+        for part in range(2):
+            send_sketch(dz, part).wait()
 
     def across(k):
-        return [SK[r, k * tiles:(k + 1) * tiles, :] for r in range(replicas)]
+        return [
+            jnp.concatenate(
+                [SK[r, part, k * pair:(k + 1) * pair, :] for part in range(2)], axis=0)
+            for r in range(replicas)
+        ]
 
     local = across(0)
     common = functools.reduce(jnp.maximum, local)
@@ -319,34 +350,15 @@
     weight = 1.0 / added(moments[0])
     level = clip_fraction([added(value) * weight for value in rebase(moments, ratio)])
     level = common * level
-    inverse = 1.0 / common
-
     for l in range(tiles):
-        lanes = slice(l * LANES, (l + 1) * LANES)
-        bound = level[l:l + 1]
-        factor = inverse[l:l + 1]
-
-        def finish(i, _):
-            part = pl.ds(pl.multiple_of(i * ROWS, ROWS), ROWS)
-            h = jnp.minimum(jnp.maximum(H[part, lanes], -bound), bound)
-            RES[part, lanes] = (h * factor).astype(jnp.bfloat16)
-            return 0
-
-        lax.fori_loop(0, rows // ROWS, finish, 0)
-
-    mine = pl.ds(pl.multiple_of(me * width, width), width)
-
-    def send_result(i):
-        j = other(*alls[i])
-        return pltpu.make_async_remote_copy(
-            src_ref=RES.at[block(j), :], dst_ref=out.at[:, mine],
-            send_sem=r_send.at[i], recv_sem=r_recv.at[i],
-            device_id=(j, z), device_id_type=MESH)
-
+        LS[0:1, l * LANES:(l + 1) * LANES] = level[l:l + 1]
+        LS[1:2, l * LANES:(l + 1) * LANES] = common[l:l + 1]
+    for i in range(len(alls)):
+        send_hidden(i).wait()
+    keep_hidden.wait()
     for i in range(len(alls))[::-1]:
-        send_result(i).start()
-    keep = pltpu.make_async_copy(RES.at[block(me), :], out.at[:, mine], own_sem)
-    keep.start()
+        send_level(i).start()
+    keep_level.start()
 
     def drain(ch, _):
         for i in range(len(combos)):
@@ -357,9 +369,9 @@
     lax.fori_loop(0, chunks, drain, 0)
     for i in range(len(combos)):
         send_filled(i).wait_send()
-    keep.wait()
+    keep_level.wait()
     for i in range(len(alls)):
-        send_result(i).wait()
+        send_level(i).wait()
 
 
 def shards(tokens, routes, gate_weight, up_weight):
@@ -374,12 +386,16 @@
     tiles = width // LANES
     bf16, f32 = jnp.bfloat16, jnp.float32
     dma = pltpu.SemaphoreType.DMA
-    anywhere = pl.BlockSpec(memory_space=pl.ANY)
-    return pl.pallas_call(
+    offchip = pl.BlockSpec(memory_space=pltpu.HBM)
+    onchip = pl.BlockSpec(memory_space=pltpu.VMEM)
+    hidden, levels = pl.pallas_call(
         functools.partial(kernel, devices, replicas, chunks),
-        out_shape=jax.ShapeDtypeStruct((CAP, devices * width), bf16),
-        in_specs=[anywhere] * 4,
-        out_specs=anywhere,
+        out_shape=(
+            jax.ShapeDtypeStruct((CAP, devices * width), f32),
+            jax.ShapeDtypeStruct((2, devices * width), f32),
+        ),
+        in_specs=[offchip] * 4,
+        out_specs=(onchip, onchip),
         scratch_shapes=[
             pltpu.VMEM((chunks, count, CHUNK), bf16),
             pltpu.VMEM((routes.shape[1], count), jnp.int32),
@@ -393,19 +409,22 @@
             pltpu.VMEM((rows, width), f32),
             pltpu.VMEM((rows, width), f32),
             pltpu.VMEM((rows, width), f32),
-            pltpu.VMEM((replicas, KMOM * tiles, LANES), f32),
+            pltpu.VMEM((replicas, 2, KMOM * tiles // 2, LANES), f32),
             pltpu.VMEM((replicas, 8, LANES), f32),
-            pltpu.VMEM((rows, width), bf16),
+            pltpu.VMEM((2, width), f32),
             dma((chunks,)), dma(()), dma((chunks,)), dma((chunks,)),
             dma((chunks, near)), dma((chunks, near)), dma((near,)), dma((near,)),
             dma((chunks,)), dma((chunks,)), dma((2,)),
+            dma((replicas - 1, 2)), dma((replicas - 1, 2)),
             dma((replicas - 1,)), dma((replicas - 1,)),
-            dma((replicas - 1,)), dma((replicas - 1,)),
-            dma((devices - 1,)), dma((devices - 1,)), dma(()),
+            dma((devices - 1,)), dma((devices - 1,)),
+            dma((devices - 1,)), dma((devices - 1,)), dma((2,)),
         ],
         compiler_params=pltpu.CompilerParams(
-            collective_id=0, has_side_effects=True, vmem_limit_bytes=60 * 1024 * 1024),
+            collective_id=0, has_side_effects=True, vmem_limit_bytes=62 * 1024 * 1024),
     )(tokens, routes.T, gate_weight, up_weight)
+    level, ceiling = levels[0:1], levels[1:2]
+    return (jnp.minimum(jnp.maximum(hidden, -level), level) / ceiling).astype(bf16)
 
 
 def solution(mesh):

time: 30.5 us -> 33.9 us (1.11)
  other arithmetic: 0 us -> 2.52 us
  Pallas kernels: 28.8 us -> 31.1 us
  local copies, waits for them, and re-layouts: 1.57 us -> 0 us
    pallas_call x1, Pallas kernels: 28.8 us -> 31.1 us  [shards(): pl.pallas_call(functools.partial(kernel, devices, replicas, chunks), out_...]
    convert_element_type x0 -> x1, other arithmetic: none -> 1.65 us  [shards(): (jnp.minimum(jnp.maximum(hidden, -level), level) / ceiling).astype(bf16)]
    unnamed x1 -> x0, local copies, waits for them, and re-layouts: 1.57 us -> none
    neg x0 -> x1, other arithmetic: none -> 0.87 us  [shards(): -level]
where the time goes in v2:
time: 33.9 us; the launch traced here: 33.7 us
  Pallas kernels  31.1 us (92%)
  other arithmetic  2.52 us (7%)
    pallas_call x1, Pallas kernels, shards(): pl.pallas_call(functools.partial(kernel, devices, replicas, chunks), out_...  31.1 us
    convert_element_type x1, other arithmetic, shards(): (jnp.minimum(jnp.maximum(hidden, -level), level) / ceiling).astype(bf16)  1.65 us
    neg x1, other arithmetic, shards(): -level  0.87 us

profile of v2, /device:TPU:0, one launch (start us, length us, event | category | flops | bytes accessed | tf_op | source)
XLA Modules:
  0.0 33.7 jit_solution(15757649182644341850)
XLA Ops:
  0.0 31.1 %shard_map.46 = (f32[16,4096]{1,0:T(8,128)}, f32[2,4096]{1,0:T(2,128)}) custom-call(bf16[256,7168]{1,0:T(8,128)(2,1)} %tok.1, s32[8,256]{1,0:T(8,128)} %bitcast.7, bf16[7168,512]{1,0:T(8,128)(2,1)} %wg.1, bf16[7168,512]{1,0:T(8,128)(2,1)} %wu.1), custom_call_target="tpu_custom_call" | custom-call | tf_op jit(solution)/shard_map/pallas_call | solution.py:391
  31.1 0.9 %slice_negate_fusion = (f32[1,4096]{1,0:T(1,128)S(1)}, f32[1,4096]{1,0:T(1,128)S(1)}, f32[1,4096]{1,0:T(1,128)S(1)}) fusion(f32[2,4096]{1,0:T(2,128)} %get-tuple-element.8), kind=kLoop, calls=%fused_computation.1 | loop fusion | flops 4096 | bytes 81920 | tf_op jit(solution)/shard_map/neg | solution.py:427
  32.0 1.6 %divide_convert_fusion = bf16[16,4096]{1,0:T(8,128)(2,1)} fusion(f32[16,4096]{1,0:T(8,128)} %get-tuple-element.7, f32[4096]{0:T(1024)S(1)} %bitcast.5, f32[4096]{0:T(1024)S(1)} %bitcast.6, f32[4096]{0:T(1024)S(1)} %bitcast.4), kind=kLoop, calls=%fused_computation | loop fusion | flops 262144 | bytes 442368 | tf_op jit(solution)/shard_map/convert_element_type | solution.py:427

commit v3 on v1

--- a/solution.py
+++ b/solution.py
@@ -379,7 +379,7 @@
         functools.partial(kernel, devices, replicas, chunks),
         out_shape=jax.ShapeDtypeStruct((CAP, devices * width), bf16),
         in_specs=[anywhere] * 4,
-        out_specs=anywhere,
+        out_specs=pl.BlockSpec(memory_space=pltpu.VMEM),
         scratch_shapes=[
             pltpu.VMEM((chunks, count, CHUNK), bf16),
             pltpu.VMEM((routes.shape[1], count), jnp.int32),
@@ -404,7 +404,7 @@
             dma((devices - 1,)), dma((devices - 1,)), dma(()),
         ],
         compiler_params=pltpu.CompilerParams(
-            collective_id=0, has_side_effects=True, vmem_limit_bytes=60 * 1024 * 1024),
+            collective_id=0, has_side_effects=True, vmem_limit_bytes=53 * 1024 * 1024),
     )(tokens, routes.T, gate_weight, up_weight)
 
 

time: 30.5 us -> 30 us (0.984)
    unnamed x1 -> x3, local copies, waits for them, and re-layouts: 1.57 us -> 1.35 us
where the time goes in v3:
time: 30 us; the launch traced here: 29.9 us
  Pallas kernels  28.5 us (95%)
  local copies, waits for them, and re-layouts  1.35 us (4%)
    pallas_call x1, Pallas kernels, shards(): pl.pallas_call(functools.partial(kernel, devices, replicas, chunks), out_...  28.5 us
    unnamed x3, local copies, waits for them, and re-layouts  1.35 us

profile of v3, /device:TPU:0, one launch (start us, length us, event | category | flops | bytes accessed | tf_op | source)
XLA Modules:
  0.0 29.9 jit_solution(3883478165891314994)
XLA Ops:
  0.0 0.0 copy-start
  0.0 0.7 %copy-done = s32[256,8]{0,1:T(8,128)S(1)} copy-done((s32[256,8]{0,1:T(8,128)S(1)}, s32[256,8]{0,1:T(8,128)}, u32[]{:S(2)}) %copy-start) | copy-done | bytes 8216
  0.7 28.5 %shard_map.46 = bf16[16,4096]{1,0:T(8,128)(2,1)S(1)} custom-call(bf16[256,7168]{1,0:T(8,128)(2,1)} %tok.1, s32[8,256]{1,0:T(8,128)S(1)} %bitcast.1, bf16[7168,512]{1,0:T(8,128)(2,1)} %wg.1, bf16[7168,512]{1,0:T(8,128)(2,1)} %wu.1), custom_call_target="tpu_custom_call" | custom-call | tf_op jit(solution)/shard_map/pallas_call | solution.py:378
  29.2 0.7 %copy.6 = bf16[16,4096]{1,0:T(8,128)(2,1)} copy(bf16[16,4096]{1,0:T(8,128)(2,1)S(1)} %shard_map.46) | data formatting | bytes 262144
Async XLA Ops:
  0.0 0.7 %copy-start = (s32[256,8]{0,1:T(8,128)S(1)}, s32[256,8]{0,1:T(8,128)}, u32[]{:S(2)}) copy-start(s32[256,8]{0,1:T(8,128)} %param.5) | copy-start | bytes 24580
